TPU v7x, 256 devices: a whole 4x4x8 slice. The times are simulated.
256 devices in a mesh: seq: 64 (over z, y, core), tp: 4 (over x).
Axes of the slice: x: 4, y: 4, z: 8, core: 2. Of those that a mesh axis runs over, the one named last changes fastest.
Arguments:
- tokens: bfloat16 [128, 1536], replicated, may hold values from -6 to 6
- attn_gain: float32 [1536], replicated, may hold values from 0.25 to 1.75
- qkv_weight: bfloat16 [1536, 2560], P(None, 'tp'), may hold values from -0.15625 to 0.15625
- out_weight: bfloat16 [1536, 1536], P(None, 'tp'), may hold values from -0.15625 to 0.15625
- moe_gain: float32 [1536], P('tp'), may hold values from 0.25 to 1.75
- router_weight: bfloat16 [1536, 40], P('tp'), may hold values from -0.3125 to 0.3125
- expert_gate: bfloat16 [40, 1536, 512], P(None, 'tp', 'seq'), may hold values from -0.15625 to 0.15625
- expert_up: bfloat16 [40, 1536, 512], P(None, 'tp', 'seq'), may hold values from -0.15625 to 0.15625
- expert_down: bfloat16 [40, 512, 1536], P(None, 'seq', 'tp'), may hold values from -0.375 to 0.375
- cache_keys: bfloat16 [32, 2048, 512], P(None, 'seq', 'tp'), may hold values from -240 to 240, as said below
- cache_values: bfloat16 [32, 2048, 512], P(None, 'seq', 'tp'), may hold values from -8 to 8
- lengths: int32 [32], replicated, may hold values from 1 to 32768, as said below
- routes: int32 [128, 8], replicated, may hold values from 0 to 39, all different within a row
Outputs:
- layer_out: bfloat16 [128, 1536], P(None, 'tp')
Inputs may be any that keep to these rules, and one draw needn't show every extreme that they name: `lengths`: one request has exactly 32768 cached positions. `cache_keys`: cached keys are already rotated.
All inputs are finite; a program needn't handle non-finite values.
Results may differ from a plain program's by a relative error of at most 0.014.
Values may be sent and summed in bfloat16 or wider, within the bound.
No kernel may reach another device: no remote copies, remote signals or barrier semaphores. Data moves between devices by JAX's collectives and lax.ppermute only.
A program may use at most 128 MiB of HBM per device.

v0:
```python
import jax
import jax.numpy as jnp
from jax import lax
from jax.sharding import PartitionSpec as P

D = 1536
HEAD = 64
EXPERTS = 40
SINK = 4
NEW = 4
GROUP = 3
EPSILON = 1e-06
ROPE_BASE = 10000.0
FLOOR_SCORE = -1e30


def joined(shard, axis, combine):
    everything = jax.tree.map(lambda part: lax.all_gather(part, axis), shard)
    initial = jax.tree.map(lambda part: part[0], everything)

    def lap(k, so_far):
        return combine(so_far, jax.tree.map(lambda part: part[k], everything))

    return lax.fori_loop(1, lax.axis_size(axis), lap, initial)


def rms_scale(values, gain):
    return values * lax.rsqrt(jnp.mean(values * values, axis=-1, keepdims=True) + EPSILON) * gain


def rotate(values, places):
    half_dim = values.shape[-1] // 2
    freqs = jnp.exp(-jnp.log(ROPE_BASE) * jnp.arange(half_dim, dtype=jnp.float32) / half_dim)
    angles = places.reshape((-1,) + (1,) * (values.ndim - 1)) * freqs
    cosine = jnp.cos(angles)
    sine = jnp.sin(angles)
    first = values[..., :half_dim]
    second = values[..., half_dim:]
    return jnp.concatenate(
        [first * cosine - second * sine, first * sine + second * cosine], axis=-1
    )


def visible(slots, lengths, window):
    lens = lengths[:, None]
    slot_row = slots[None, :]
    live = slot_row < lens
    older = lens - 1 - jnp.mod(lens - 1 - slot_row, window)
    placed = jnp.where(slot_row < SINK, slot_row, older)
    offsets = jnp.arange(NEW, dtype=jnp.int32)
    inside = (slot_row[:, None, :] < SINK) | (
        placed[:, None, :] >= lens[:, :, None] + offsets[None, :, None] - window
    )
    return live[:, None, :] & inside


def combine_parts(earlier, later):
    top_a, mass_a, weighted_a = earlier
    top_b, mass_b, weighted_b = later
    top_both = jnp.maximum(top_a, top_b)
    factor_a = jnp.exp(top_a - top_both)
    factor_b = jnp.exp(top_b - top_both)
    return (
        top_both,
        mass_a * factor_a + mass_b * factor_b,
        weighted_a * factor_a[..., None] + weighted_b * factor_b[..., None],
    )


def on_device(
    tokens,
    attn_gain,
    qkv_weight,
    out_weight,
    moe_gain,
    router_weight,
    expert_gate,
    expert_up,
    expert_down,
    cache_keys,
    cache_values,
    lengths,
    routes,
):
    seq_count = lax.axis_size("seq")
    seq_index = lax.axis_index("seq")
    tp_index = lax.axis_index("tp")
    token_count = tokens.shape[0]
    requests = cache_keys.shape[0]
    slot_count = cache_keys.shape[1]
    window = slot_count * seq_count - SINK
    local_kv = cache_keys.shape[2] // HEAD
    token_full = tokens.astype(jnp.float32)
    normed = rms_scale(token_full, attn_gain).astype(jnp.bfloat16)
    projected = jnp.dot(normed, qkv_weight, preferred_element_type=jnp.float32)
    projected = projected.reshape(token_count, local_kv, GROUP + 2, HEAD)
    places = (
        (lengths[:, None] + jnp.arange(NEW, dtype=jnp.int32)[None, :])
        .reshape(token_count)
        .astype(jnp.float32)
    )
    queries = rotate(projected[:, :, :GROUP], places).astype(jnp.bfloat16)
    new_keys = rotate(projected[:, :, GROUP], places).astype(jnp.bfloat16)
    new_values = projected[:, :, GROUP + 1].astype(jnp.bfloat16)
    query_b = queries.reshape(requests, NEW, local_kv, GROUP, HEAD)
    key_new = new_keys.reshape(requests, NEW, local_kv, HEAD)
    value_new = new_values.reshape(requests, NEW, local_kv, HEAD)
    slots = seq_index * slot_count + jnp.arange(slot_count, dtype=jnp.int32)
    seen = visible(slots, lengths, window)[:, :, None, None, :]
    factor = 1.0 / HEAD**0.5
    key_old = cache_keys.reshape(requests, slot_count, local_kv, HEAD)
    value_old = cache_values.reshape(requests, slot_count, local_kv, HEAD)
    old_scores = (
        jnp.einsum("rtgqd,rsgd->rtgqs", query_b, key_old, preferred_element_type=jnp.float32)
        * factor
    )
    new_scores = (
        jnp.einsum("rtgqd,rugd->rtgqu", query_b, key_new, preferred_element_type=jnp.float32)
        * factor
    )
    causal = jnp.arange(NEW)[:, None] >= jnp.arange(NEW)[None, :]
    own_mask = causal[None, :, None, None, :] & (seq_index == 0)
    old_masked = jnp.where(seen, old_scores, FLOOR_SCORE)
    new_masked = jnp.where(own_mask, new_scores, FLOOR_SCORE)
    top_score = jnp.maximum(jnp.max(old_masked, axis=-1), jnp.max(new_masked, axis=-1))
    old_weights = jnp.where(seen, jnp.exp(old_masked - top_score[..., None]), 0.0)
    new_weights = jnp.where(own_mask, jnp.exp(new_masked - top_score[..., None]), 0.0)
    mass = jnp.sum(old_weights, axis=-1) + jnp.sum(new_weights, axis=-1)
    weighted = jnp.einsum(
        "rtgqs,rsgd->rtgqd", old_weights, value_old.astype(jnp.float32)
    ) + jnp.einsum("rtgqu,rugd->rtgqd", new_weights, value_new.astype(jnp.float32))
    top_score, mass, weighted = joined((top_score, mass, weighted), "seq", combine_parts)
    attended = (weighted / mass[..., None]).reshape(token_count, -1).astype(jnp.bfloat16)
    feature_part = out_weight.shape[1]
    attn_out = jnp.dot(
        lax.all_gather(attended, "tp", axis=1, tiled=True),
        out_weight,
        preferred_element_type=jnp.float32,
    )
    residual = (
        lax.dynamic_slice_in_dim(token_full, tp_index * feature_part, feature_part, 1) + attn_out
    )
    gained = residual * moe_gain
    squares_local = jnp.sum(residual * residual, axis=-1)
    router_f = router_weight.astype(jnp.float32)
    squares_total = lax.psum(squares_local, "tp")
    scale = lax.rsqrt(squares_total / D + EPSILON)
    logits = lax.psum(
        jnp.dot(gained * scale[:, None], router_f, precision=lax.Precision.HIGHEST), "tp"
    )
    moe_in = (gained * scale[:, None]).astype(jnp.bfloat16)
    chosen = jnp.take_along_axis(logits, routes, axis=1)
    gate_prob = jax.nn.softmax(chosen, axis=-1)
    gate_part = jnp.einsum("td,edf->tef", moe_in, expert_gate, preferred_element_type=jnp.float32)
    up_part = jnp.einsum("td,edf->tef", moe_in, expert_up, preferred_element_type=jnp.float32)
    gate_pick = jnp.take_along_axis(gate_part, routes[:, :, None], axis=1)
    up_pick = jnp.take_along_axis(up_part, routes[:, :, None], axis=1)
    gate_sum, up_sum = (
        lax.psum(gate_pick.astype(jnp.bfloat16), "tp").astype(jnp.float32),
        lax.psum(up_pick.astype(jnp.bfloat16), "tp").astype(jnp.float32),
    )
    activated = (jax.nn.silu(gate_sum) * up_sum).astype(jnp.bfloat16)
    scaled = (gate_prob[:, :, None] * activated.astype(jnp.float32)).astype(jnp.bfloat16)
    onehot = (routes[:, :, None] == jnp.arange(EXPERTS, dtype=jnp.int32)[None, None, :]).astype(
        jnp.bfloat16
    )
    spread = jnp.einsum("tke,tkf->tef", onehot, scaled, preferred_element_type=jnp.float32).astype(
        jnp.bfloat16
    )
    moe_part = jnp.einsum("tef,efd->td", spread, expert_down, preferred_element_type=jnp.float32)
    moe_out = lax.psum(moe_part, "seq")
    return (residual + moe_out).astype(jnp.bfloat16)


def solution(mesh):
    in_specs = (
        P(),
        P(),
        P(None, "tp"),
        P(None, "tp"),
        P("tp"),
        P("tp", None),
        P(None, "tp", "seq"),
        P(None, "tp", "seq"),
        P(None, "seq", "tp"),
        P(None, "seq", "tp"),
        P(None, "seq", "tp"),
        P(),
        P(),
    )
    out_specs = P(None, "tp")
    return jax.shard_map(
        on_device, mesh=mesh, in_specs=in_specs, out_specs=out_specs, check_vma=False
    )
```

profile of v0, /device:TPU:2, one launch (start us, length us, event | category | flops | bytes accessed | tf_op | source)
XLA Modules:
  0.0 648.5 jit_solution(3661215171053748610)
XLA Ops:
  8.1 1.2 multiply_reduce_fusion
  9.3 2.0 fusion.11
  13.8 1.2 reshape.397
  16.1 1.5 fusion.59
  18.1 1.2 fusion.4
  21.6 61.3 %all-gather.1 = f32[2048,4,2,3]{1,2,3,0:T(2,128)S(1)} all-gather(f32[32,4,2,3]{1,2,3,0:T(2,128)S(1)} %copy.167), channel_id=3, replica_groups=mesh['seq'=64,'tp'=4] {'seq'}, dimensions={0}, use_global_device_ids=true | all-gather | bytes 199680 | tf_op jit(solution)/shard_map/all_gather | solution.py:18
  82.9 2.7 copy-done.1
  85.6 8.5 %copy.178 = f32[64,32,4,2,3]{1,3,4,2,0:T(2,128)} copy(f32[64,32,4,2,3]{2,3,4,1,0:T(2,128)} %bitcast.82) | data formatting | bytes 393216 | tf_op jit(solution)/shard_map/while | solution.py:24
  94.2 60.6 %all-gather = f32[2048,4,2,3]{1,2,3,0:T(2,128)S(1)} all-gather(f32[32,4,2,3]{1,2,3,0:T(2,128)S(1)} %copy.166), channel_id=2, replica_groups=mesh['seq'=64,'tp'=4] {'seq'}, dimensions={0}, use_global_device_ids=true | all-gather | bytes 199680 | tf_op jit(solution)/shard_map/all_gather | solution.py:18
  154.8 2.7 copy-done.2
  157.6 8.5 %copy.177 = f32[64,32,4,2,3]{1,3,4,2,0:T(2,128)} copy(f32[64,32,4,2,3]{2,3,4,1,0:T(2,128)} %bitcast.83) | data formatting | bytes 393216 | tf_op jit(solution)/shard_map/while | solution.py:24
  168.4 199.7 %while.19 = (s32[]{:T(128)}, f32[32,4,2,3]{0,2,3,1:T(2,128)S(1)}, f32[32,4,2,3]{0,2,3,1:T(2,128)S(1)}, f32[32,4,2,3,64]{4,3,2,1,0:T(4,128)S(1)}, f32[64,32,4,2,3...) while((s32[]{:T(128)}, f32[32,4,2,3]{0,2,3,1:T(2,128)S(1)}, ...), condition=%wide.region_6.7_spmd, body=%wide.region_5.6_spmd.sunk | while | flops 152069 | bytes 1026199 | solution.py:24
  169.6 1.0 constant_dynamic-slice_fusion.2
  172.7 1.0 constant_dynamic-slice_fusion.2
  175.9 1.0 constant_dynamic-slice_fusion.2
  179.1 1.0 constant_dynamic-slice_fusion.2
  182.2 1.0 constant_dynamic-slice_fusion.2
  185.4 1.0 constant_dynamic-slice_fusion.2
  188.6 1.0 constant_dynamic-slice_fusion.2
  191.7 1.0 constant_dynamic-slice_fusion.2
  194.9 1.0 constant_dynamic-slice_fusion.2
  198.1 1.0 constant_dynamic-slice_fusion.2
  201.3 1.0 constant_dynamic-slice_fusion.2
  204.4 1.0 constant_dynamic-slice_fusion.2
  207.6 1.0 constant_dynamic-slice_fusion.2
  210.8 1.0 constant_dynamic-slice_fusion.2
  213.9 1.0 constant_dynamic-slice_fusion.2
  217.1 1.0 constant_dynamic-slice_fusion.2
  220.3 1.0 constant_dynamic-slice_fusion.2
  223.4 1.0 constant_dynamic-slice_fusion.2
  226.6 1.0 constant_dynamic-slice_fusion.2
  229.8 1.0 constant_dynamic-slice_fusion.2
  368.9 13.3 %all_gather.21 = bf16[128,1536]{1,0:T(8,128)(2,1)S(1)} all-gather(bf16[128,384]{1,0:T(8,128)(2,1)S(1)} %convert_element_type.75), channel_id=1, replica_groups=mesh['seq'=64,'tp'=4] {'tp'}, dimensions={1}, use_global_device_ids=true | all-gather | bytes 491520 | tf_op jit(solution)/shard_map/all_gather | solution.py:136
  382.2 1.8 multiply_reduce_fusion.1
  384.0 8.0 %psum.35 = f32[128]{0:T(128)S(1)} all-reduce(f32[128]{0:T(128)S(1)} %get-tuple-element.256), channel_id=1, replica_groups=mesh['seq'=64,'tp'=4] {'tp'}, use_global_device_ids=true, to_apply=%region_8.9 | all-reduce | flops 128 | bytes 1024 | tf_op jit(solution)/shard_map/psum | solution.py:146
  393.5 1.8 copy.191
  395.3 10.5 %gather_fusion.2 = bf16[1024,8]{1,0:T(8,128)(2,1)} fusion(bf16[128,40,8]{2,1,0:T(8,128)(2,1)S(1)} %copy.191, s32[1024]{0:T(1024)S(1)} %reshape.431), kind=kCustom, calls=%fused_computation.1.clone | custom fusion | bytes 40960 | tf_op jit(solution)/shard_map/jit(take_along_axis)/gather | solution.py:157
  405.8 1.7 copy.193
  407.5 1.9 fusion.20
  409.4 1.8 copy.186
  411.2 10.5 %gather_fusion.1 = bf16[1024,8]{1,0:T(8,128)(2,1)} fusion(bf16[128,40,8]{2,1,0:T(8,128)(2,1)S(1)} %copy.186, s32[1024]{0:T(1024)S(1)} %reshape.431), kind=kCustom, calls=%fused_computation.clone | custom fusion | bytes 40960 | tf_op jit(solution)/shard_map/jit(take_along_axis)/gather | solution.py:156
  421.7 1.1 copy.188
  422.8 1.1 fusion.29
  423.9 15.9 %psum.36 = f32[128,40]{0,1:T(8,128)S(1)} all-reduce(f32[128,40]{0,1:T(8,128)S(1)} %fusion.29), channel_id=1, replica_groups=mesh['seq'=64,'tp'=4] {'tp'}, use_global_device_ids=true, to_apply=%region_9.10 | all-reduce | flops 5120 | bytes 40960 | tf_op jit(solution)/shard_map/psum | solution.py:148
  439.8 7.0 %gather_fusion = f32[1024]{0:T(1024)S(1)} fusion(f32[128,40]{0,1:T(8,128)S(1)} %psum.36, s32[1024]{0:T(1024)S(1)} %reshape.411), kind=kCustom, calls=%fused_computation.2 | custom fusion | bytes 16384 | tf_op jit(solution)/shard_map/jit(take_along_axis)/gather | solution.py:152
  447.1 14.5 %all-reduce = (bf16[128,8,8]{0,2,1:T(8,128)(2,1)S(1)}, bf16[128,8,8]{0,2,1:T(8,128)(2,1)S(1)}) all-reduce(bf16[128,8,8]{0,2,1:T(8,128)(2,1)S(1)} %get-tuple-element.247, bf16[128,8,8]{0,2,1:T(8,128)(2,1)S(1)} %get-tuple-element.246), channel_id=1, replica_groups=mesh['seq'=64,'tp'=4] {'tp'}, use_global_device_ids=true, to_apply=%region_13.15 | all-reduce | flops 16384 | bytes 65536 | tf_op jit(solution)/shard_map/psum | solution.py:160
  463.4 176.7 %all-reduce.3.cloned.1.call-done = f32[128,384]{1,0:T(8,128)} async-done(((f32[128,384]{1,0:T(8,128)}), f32[128,384]{1,0:T(8,128)}) %all-reduce.3.cloned.1.call-update) | async-done | bytes 196624 | tf_op jit(solution)/shard_map/psum | solution.py:171
  640.1 1.6 add_convert_fusion
  (392 shorter events, 190.9 us)
Async XLA Ops:
  6.5 2.7 copy-start
  6.5 4.7 copy-start.15
  6.5 160.7 %all-gather.5.cloned.1.call-start = ((), (), s32[]{:S(2)}) async-start(), calls=%async_computation.1 | async-start | bytes 25559040 | tf_op jit(solution)/shard_map/all_gather | solution.py:18
  9.3 2.8 copy-start.6
  15.1 1.0 copy-start.10
  15.1 1.0 copy-start.11
  16.1 2.0 copy-start.4
  18.1 1.3 copy-start.3
  18.1 2.7 copy-start.5
  19.4 620.7 %all-reduce.3.cloned.1.call-start = ((), (), s32[]{:S(2)}) async-start(), calls=%async_computation | async-start | bytes 393216 | tf_op jit(solution)/shard_map/psum | solution.py:171
  82.9 2.7 copy-start.1
  154.8 2.7 copy-start.2
  157.6 8.6 %copy-start.9 = (s32[128,8]{0,1:T(8,128)S(1)}, s32[128,8]{0,1:T(8,128)}, u32[]{:S(2)}) copy-start(s32[128,8]{0,1:T(8,128)} %param.29) | copy-start | bytes 12292
  368.2 24.4 %copy-start.7 = (bf16[40,384,8]{1,2,0:T(8,128)(2,1)S(1)}, bf16[40,384,8]{1,2,0:T(8,128)(2,1)}, u32[]{:S(2)}) copy-start(bf16[40,384,8]{1,2,0:T(8,128)(2,1)} %param.24) | copy-start | bytes 737284
  368.2 24.4 %copy-start.13 = (f32[384]{0:T(512)S(1)}, f32[384]{0:T(512)}, u32[]{:S(2)}) copy-start(f32[384]{0:T(512)} %param.21) | copy-start | bytes 4612
  392.0 0.5 copy-start.14
  439.8 7.3 %copy-start.12 = (bf16[128,8,8]{0,2,1:T(8,128)(2,1)S(1)}, bf16[128,8,8]{0,2,1:T(8,128)(2,1)}, u32[]{:S(2)}) copy-start(bf16[128,8,8]{0,2,1:T(8,128)(2,1)} %copy.193) | copy-start | bytes 49156
  439.8 7.3 %copy-start.16 = (pred[128,8]{0,1:T(8,128)(4,1)S(1)}, pred[128,8]{0,1:T(8,128)(4,1)}, u32[]{:S(2)}) copy-start(pred[128,8]{0,1:T(8,128)(4,1)} %and_bitcast_fusion) | copy-start | bytes 3076
  446.8 15.6 %copy-start.8 = (bf16[40,8,384]{2,1,0:T(8,128)(2,1)S(1)}, bf16[40,8,384]{2,1,0:T(8,128)(2,1)}, u32[]{:S(2)}) copy-start(bf16[40,8,384]{2,1,0:T(8,128)(2,1)} %param.25) | copy-start | bytes 737284
Sparse Core Ops, SparseCore 0:
  19.5 144.7 all-gather.4
  463.5 176.5 all-reduce.2
where the time goes:
time: 659 us; the launch traced here: 649 us
  waiting for transfers between devices  177 us (27%)
  blocking collectives  174 us (26%)
  local copies, waits for them, and re-layouts  150 us (23%)
  other arithmetic  119 us (18%)
  between operations  13.9 us (2%)
  matrix products  12.6 us (2%)
    psum x1, waiting for transfers between devices, on_device(): moe_out = lax.psum(moe_part, 'seq')  177 us
    all_gather x2, blocking collectives, joined(): everything = jax.tree.map(lambda part: lax.all_gather(part, axis), shard)  122 us
    dynamic_slice x63, local copies, waits for them, and re-layouts, lap(): return combine(so_far, jax.tree.map(lambda part: part[k], everything))  65.7 us
    add x63, other arithmetic, combine_parts(): weighted_a * factor_a[..., None] + weighted_b * factor_b[..., None]  62.8 us
    add x63, other arithmetic, combine_parts(): mass_a * factor_a + mass_b * factor_b  48.3 us
    while x6, local copies, waits for them, and re-layouts, joined(): return lax.fori_loop(1, lax.axis_size(axis), lap, initial)  17.5 us
    psum x1, blocking collectives, on_device(): lax.psum(jnp.dot(gained * scale[:, None], router_f, precision=lax.Precisi...  15.9 us
    psum x1, blocking collectives, on_device(): lax.psum(up_pick.astype(jnp.bfloat16), 'tp').astype(jnp.float32)  14.5 us
  transfers between devices with their start and end apart: 2, of which 1 were waited for; matrix products, arithmetic and copies ran while one was open for 3% of the time, Pallas kernels for 0%

commit v1 on v0

--- a/solution.py
+++ b/solution.py
@@ -82,6 +82,10 @@
     lengths,
     routes,
 ):
+
+    def _trace_pieces_all(array_in, ax_name):
+        return jnp.sum(lax.all_gather(array_in, ax_name), 0)
+
     seq_count = lax.axis_size("seq")
     seq_index = lax.axis_index("seq")
     tp_index = lax.axis_index("tp")
@@ -168,7 +172,7 @@
         jnp.bfloat16
     )
     moe_part = jnp.einsum("tef,efd->td", spread, expert_down, preferred_element_type=jnp.float32)
-    moe_out = lax.psum(moe_part, "seq")
+    moe_out = _trace_pieces_all(moe_part, "seq")
     return (residual + moe_out).astype(jnp.bfloat16)
 
 

time: 659 us -> 553 us (0.84)
  the two profiles are of different devices: /device:TPU:2 before, /device:TPU:1 now
where the time goes in v1:
time: 553 us; the launch traced here: 543 us
  blocking collectives  164 us (30%)
  local copies, waits for them, and re-layouts  133 us (24%)
  other arithmetic  121 us (22%)
  waiting for transfers between devices  99 us (18%)
  between operations  13.9 us (3%)
  matrix products  8.35 us (2%)
    all_gather x2, blocking collectives, joined(): everything = jax.tree.map(lambda part: lax.all_gather(part, axis), shard)  123 us
    all_gather x1, waiting for transfers between devices, _trace_pieces_all(): return jnp.sum(lax.all_gather(array_in, ax_name), 0)  98.9 us
    dynamic_slice x63, local copies, waits for them, and re-layouts, lap(): return combine(so_far, jax.tree.map(lambda part: part[k], everything))  65.7 us
    add x63, other arithmetic, combine_parts(): weighted_a * factor_a[..., None] + weighted_b * factor_b[..., None]  61.8 us
    add x63, other arithmetic, combine_parts(): mass_a * factor_a + mass_b * factor_b  48.4 us
    while x6, local copies, waits for them, and re-layouts, joined(): return lax.fori_loop(1, lax.axis_size(axis), lap, initial)  17.7 us
    psum x1, blocking collectives, on_device(): lax.psum(up_pick.astype(jnp.bfloat16), 'tp').astype(jnp.float32)  12.1 us
  transfers between devices with their start and end apart: 2, of which 1 were waited for; matrix products, arithmetic and copies ran while one was open for 4% of the time, Pallas kernels for 0%

profile of v1, /device:TPU:1, one launch (start us, length us, event | category | flops | bytes accessed | tf_op | source)
XLA Modules:
  0.0 542.6 jit_solution(9062822825560332009)
XLA Ops:
  8.1 1.2 multiply_reduce_fusion
  9.3 2.0 fusion.11
  14.0 1.5 fusion.59
  16.0 1.2 fusion.4
  18.5 62.0 %all-gather.1 = f32[2048,4,2,3]{1,2,3,0:T(2,128)S(1)} all-gather(f32[32,4,2,3]{1,2,3,0:T(2,128)S(1)} %copy.167), channel_id=3, replica_groups=mesh['seq'=64,'tp'=4] {'seq'}, dimensions={0}, use_global_device_ids=true | all-gather | bytes 199680 | tf_op jit(solution)/shard_map/all_gather | solution.py:18
  80.5 2.7 copy-done.2
  83.2 8.6 %copy.178 = f32[64,32,4,2,3]{1,3,4,2,0:T(2,128)} copy(f32[64,32,4,2,3]{2,3,4,1,0:T(2,128)} %bitcast.83) | data formatting | bytes 393216 | tf_op jit(solution)/shard_map/while | solution.py:24
  91.9 61.0 %all-gather = f32[2048,4,2,3]{1,2,3,0:T(2,128)S(1)} all-gather(f32[32,4,2,3]{1,2,3,0:T(2,128)S(1)} %copy.166), channel_id=2, replica_groups=mesh['seq'=64,'tp'=4] {'seq'}, dimensions={0}, use_global_device_ids=true | all-gather | bytes 199680 | tf_op jit(solution)/shard_map/all_gather | solution.py:18
  152.9 2.7 copy-done.3
  155.7 8.6 %copy.177 = f32[64,32,4,2,3]{1,3,4,2,0:T(2,128)} copy(f32[64,32,4,2,3]{2,3,4,1,0:T(2,128)} %bitcast.84) | data formatting | bytes 393216 | tf_op jit(solution)/shard_map/while | solution.py:24
  166.1 198.8 %while.19 = (s32[]{:T(128)}, f32[32,4,2,3]{0,2,3,1:T(2,128)S(1)}, f32[32,4,2,3]{0,2,3,1:T(2,128)S(1)}, f32[32,4,2,3,64]{4,3,2,1,0:T(4,128)S(1)}, f32[64,32,4,2,3...) while((s32[]{:T(128)}, f32[32,4,2,3]{0,2,3,1:T(2,128)S(1)}, ...), condition=%wide.region_6.7_spmd, body=%wide.region_5.6_spmd.sunk | while | flops 152069 | bytes 1026199 | solution.py:24
  170.4 1.0 constant_dynamic-slice_fusion.2
  176.7 1.0 constant_dynamic-slice_fusion.2
  183.0 1.0 constant_dynamic-slice_fusion.2
  189.3 1.0 constant_dynamic-slice_fusion.2
  195.7 1.0 constant_dynamic-slice_fusion.2
  202.0 1.0 constant_dynamic-slice_fusion.2
  208.3 1.0 constant_dynamic-slice_fusion.2
  211.4 1.0 constant_dynamic-slice_fusion.2
  217.7 1.0 constant_dynamic-slice_fusion.2
  220.9 1.0 constant_dynamic-slice_fusion.2
  227.2 1.0 constant_dynamic-slice_fusion.2
  230.4 1.0 constant_dynamic-slice_fusion.2
  236.7 1.0 constant_dynamic-slice_fusion.2
  243.0 1.0 constant_dynamic-slice_fusion.2
  249.3 1.0 constant_dynamic-slice_fusion.2
  255.6 1.0 constant_dynamic-slice_fusion.2
  261.9 1.0 constant_dynamic-slice_fusion.2
  265.1 1.0 constant_dynamic-slice_fusion.2
  268.2 1.0 constant_dynamic-slice_fusion.2
  271.4 1.0 constant_dynamic-slice_fusion.2
  277.7 1.0 constant_dynamic-slice_fusion.2
  284.0 1.0 constant_dynamic-slice_fusion.2
  290.3 1.0 constant_dynamic-slice_fusion.2
  296.6 1.0 constant_dynamic-slice_fusion.2
  303.0 1.0 constant_dynamic-slice_fusion.2
  309.3 1.0 constant_dynamic-slice_fusion.2
  315.6 1.0 constant_dynamic-slice_fusion.2
  321.9 1.0 constant_dynamic-slice_fusion.2
  365.7 10.8 %all_gather.27 = bf16[128,1536]{1,0:T(8,128)(2,1)S(1)} all-gather(bf16[128,384]{1,0:T(8,128)(2,1)S(1)} %convert_element_type.75), channel_id=1, replica_groups=mesh['seq'=64,'tp'=4] {'tp'}, dimensions={1}, use_global_device_ids=true | all-gather | bytes 491520 | tf_op jit(solution)/shard_map/all_gather | solution.py:140
  376.9 7.4 %psum.28 = f32[128]{0:T(128)S(1)} all-reduce(f32[128]{0:T(128)S(1)} %get-tuple-element.256), channel_id=1, replica_groups=mesh['seq'=64,'tp'=4] {'tp'}, use_global_device_ids=true, to_apply=%region_8.9 | all-reduce | flops 128 | bytes 1024 | tf_op jit(solution)/shard_map/psum | solution.py:150
  385.3 5.8 %gather_fusion.2 = bf16[1024,8]{1,0:T(8,128)(2,1)S(1)} fusion(bf16[128,40,8]{2,1,0:T(8,128)(2,1)S(1)} %copy.191, s32[1024]{0:T(1024)S(1)} %reshape.432), kind=kCustom, calls=%fused_computation.1.clone | custom fusion | bytes 40960 | tf_op jit(solution)/shard_map/jit(take_along_axis)/gather | solution.py:161
  392.3 5.8 %gather_fusion.1 = bf16[1024,8]{1,0:T(8,128)(2,1)S(1)} fusion(bf16[128,40,8]{2,1,0:T(8,128)(2,1)S(1)} %copy.186, s32[1024]{0:T(1024)S(1)} %reshape.432), kind=kCustom, calls=%fused_computation.clone | custom fusion | bytes 40960 | tf_op jit(solution)/shard_map/jit(take_along_axis)/gather | solution.py:160
  398.7 10.9 %psum.29 = f32[128,40]{0,1:T(8,128)S(1)} all-reduce(f32[128,40]{0,1:T(8,128)S(1)} %fusion.29), channel_id=1, replica_groups=mesh['seq'=64,'tp'=4] {'tp'}, use_global_device_ids=true, to_apply=%region_9.10 | all-reduce | flops 5120 | bytes 40960 | tf_op jit(solution)/shard_map/psum | solution.py:152
  409.7 7.0 %gather_fusion = f32[1024]{0:T(1024)S(1)} fusion(f32[128,40]{0,1:T(8,128)S(1)} %psum.29, s32[1024]{0:T(1024)S(1)} %reshape.411), kind=kCustom, calls=%fused_computation.2 | custom fusion | bytes 16384 | tf_op jit(solution)/shard_map/jit(take_along_axis)/gather | solution.py:156
  416.9 12.1 %all-reduce = (bf16[128,8,8]{0,2,1:T(8,128)(2,1)S(1)}, bf16[128,8,8]{0,2,1:T(8,128)(2,1)S(1)}) all-reduce(bf16[128,8,8]{0,2,1:T(8,128)(2,1)S(1)} %get-tuple-element.247, bf16[128,8,8]{0,2,1:T(8,128)(2,1)S(1)} %get-tuple-element.246), channel_id=1, replica_groups=mesh['seq'=64,'tp'=4] {'tp'}, use_global_device_ids=true, to_apply=%region_13.15 | all-reduce | flops 16384 | bytes 65536 | tf_op jit(solution)/shard_map/psum | solution.py:164
  430.9 98.9 %all-gather.9.cloned.1.call-done = f32[8192,384]{1,0:T(8,128)} async-done(((f32[128,384]{1,0:T(8,128)}), f32[8192,384]{1,0:T(8,128)}) %all-gather.9.cloned.1.call-update) | async-done | bytes 12582928 | tf_op jit(solution)/shard_map/all_gather | solution.py:87
  529.8 5.3 reduce_sum.59
  (389 shorter events, 181.6 us)
Async XLA Ops:
  6.5 2.7 copy-start
  6.5 4.8 copy-start.14
  6.5 158.4 %all-gather.7.cloned.1.call-start = ((), (), s32[]{:S(2)}) async-start(), calls=%async_computation | async-start | bytes 25559040 | tf_op jit(solution)/shard_map/all_gather | solution.py:18
  9.3 2.8 copy-start.6
  9.3 3.3 copy-start.7
  16.0 1.3 copy-start.4
  17.2 512.6 %all-gather.9.cloned.1.call-start = ((), (), s32[]{:S(2)}) async-start(), calls=%async_computation.1 | async-start | bytes 12779520 | tf_op jit(solution)/shard_map/all_gather | solution.py:87
  80.5 2.7 copy-start.2
  152.9 2.7 copy-start.3
  155.7 8.7 %copy-start.11 = (s32[128,8]{0,1:T(8,128)S(1)}, s32[128,8]{0,1:T(8,128)}, u32[]{:S(2)}) copy-start(s32[128,8]{0,1:T(8,128)} %param.29) | copy-start | bytes 12292
  365.0 11.5 %copy-start.5 = (bf16[1536,384]{1,0:T(8,128)(2,1)S(1)}, bf16[1536,384]{1,0:T(8,128)(2,1)}, u32[]{:S(2)}) copy-start(bf16[1536,384]{1,0:T(8,128)(2,1)} %param.20) | copy-start | bytes 3538948
  365.0 19.4 %copy-start.8 = (bf16[40,384,8]{1,2,0:T(8,128)(2,1)S(1)}, bf16[40,384,8]{1,2,0:T(8,128)(2,1)}, u32[]{:S(2)}) copy-start(bf16[40,384,8]{1,2,0:T(8,128)(2,1)} %param.24) | copy-start | bytes 737284
  365.0 19.3 %copy-start.13 = (f32[384]{0:T(512)S(1)}, f32[384]{0:T(512)}, u32[]{:S(2)}) copy-start(f32[384]{0:T(512)} %param.21) | copy-start | bytes 4612
  384.7 6.7 %copy-start.9 = (bf16[40,384,8]{1,2,0:T(8,128)(2,1)S(1)}, bf16[40,384,8]{1,2,0:T(8,128)(2,1)}, u32[]{:S(2)}) copy-start(bf16[40,384,8]{1,2,0:T(8,128)(2,1)} %param.23) | copy-start | bytes 737284
  391.7 6.7 %copy-start.12 = (bf16[384,40]{0,1:T(8,128)(2,1)S(1)}, bf16[384,40]{0,1:T(8,128)(2,1)}, u32[]{:S(2)}) copy-start(bf16[384,40]{0,1:T(8,128)(2,1)} %param.22) | copy-start | bytes 92164
  416.7 13.2 %copy-start.10 = (bf16[40,8,384]{2,1,0:T(8,128)(2,1)S(1)}, bf16[40,8,384]{2,1,0:T(8,128)(2,1)}, u32[]{:S(2)}) copy-start(bf16[40,8,384]{2,1,0:T(8,128)(2,1)} %param.25) | copy-start | bytes 737284
  529.8 6.0 %copy-start.1 = (bf16[1536,640]{1,0:T(8,128)(2,1)S(1)}, bf16[1536,640]{1,0:T(8,128)(2,1)}, u32[]{:S(2)}) copy-start(bf16[1536,640]{1,0:T(8,128)(2,1)} %param.19) | copy-start | bytes 5898244
Sparse Core Ops, SparseCore 0:
  17.3 145.6 all-gather.6
  431.0 98.7 all-gather.8
